TPU v7x, 32 devices: a whole 2x2x4 slice. The times are simulated.
32 devices in a mesh: rows: 8 (over z, y), mp: 4 (over x, core).
Axes of the slice: x: 2, y: 2, z: 4, core: 2. Of those that a mesh axis runs over, the one named last changes fastest.
Arguments:
- calib: bfloat16 [512, 8192], P('rows', 'mp'), may hold values from -40 to 40
- weight: bfloat16 [8192, 8192], P('rows', 'mp'), may hold values from -6 to 6
- inverse_factor: float32 [8192, 8192], P('rows', 'mp'), may hold values from -10 to 12, as said below
- pruned_blocks: int32 [7], replicated, may hold values from 0 to 63, as said below
Outputs:
- pruned_weight: bfloat16 [8192, 8192], P('rows', 'mp')
- next_gram: float32 [8192, 8192], P('rows', 'mp')
Inputs may be any that keep to these rules, and one draw needn't show every extreme that they name: `pruned_blocks`: 7 distinct block numbers in any order; block b holds rows b * 128 to b * 128 + 127. `inverse_factor`: symmetric and positive definite.
All inputs are finite; a program needn't handle non-finite values.
Results may differ from a plain program's by a relative error of at most 0.0095.
Values may be sent and summed in bfloat16 or wider, within the bound.
A program may use at most 128 MiB of HBM per device.

v0:
```python
import jax
import jax.numpy as jnp
from jax import lax
from jax.sharding import PartitionSpec as P

BLOCK = 128


def spd_solve(chol_lower, right_side):
    forward = lax.linalg.triangular_solve(chol_lower, right_side, left_side=True, lower=True)
    return lax.linalg.triangular_solve(
        chol_lower, forward, left_side=True, lower=True, transpose_a=True
    )


def shards(calib, weight, inverse_factor, pruned_blocks):
    rows_dev = weight.shape[0]
    width_dev = weight.shape[1]
    full_width = width_dev * lax.axis_size("mp")
    row_start = lax.axis_index("rows") * rows_dev
    col_start = lax.axis_index("mp") * width_dev
    starts = pruned_blocks * BLOCK
    block_count = pruned_blocks.shape[0]
    col_pieces = []
    for slot_index in range(block_count):
        offset = starts[slot_index] - col_start
        inside = ((offset >= 0) & (offset < width_dev)).astype(jnp.float32)
        clamped = jnp.clip(offset, 0, width_dev - BLOCK)
        col_pieces.append(lax.dynamic_slice_in_dim(inverse_factor, clamped, BLOCK, 1) * inside)
    columns = lax.psum(jnp.concatenate(col_pieces, axis=1), "mp")
    weight_parts = []
    inverse_parts = []
    for slot_index in range(block_count):
        offset = starts[slot_index] - row_start
        inside = ((offset >= 0) & (offset < rows_dev)).astype(jnp.float32)
        clamped = jnp.clip(offset, 0, rows_dev - BLOCK)
        weight_parts.append(
            lax.dynamic_slice_in_dim(weight, clamped, BLOCK, 0).astype(jnp.float32) * inside
        )
        inverse_parts.append(lax.dynamic_slice_in_dim(columns, clamped, BLOCK, 0) * inside)
    kept_rows = lax.psum(jnp.concatenate(weight_parts, axis=0).astype(jnp.bfloat16), "rows").astype(
        jnp.float32
    )
    inverse_square = lax.psum(jnp.concatenate(inverse_parts, axis=0), "rows")
    chol_lower = jnp.linalg.cholesky(inverse_square)
    factors = spd_solve(chol_lower, columns.T)
    update = lax.dot_general(
        factors, kept_rows, (((0,), (0,)), ((), ())), precision=lax.Precision.HIGHEST
    )
    block_ids = (row_start + jnp.arange(rows_dev, dtype=jnp.int32)) // BLOCK
    kept_mask = 1.0 - jnp.any(block_ids[:, None] == pruned_blocks[None, :], axis=1).astype(
        jnp.float32
    )
    pruned_weight = ((weight.astype(jnp.float32) - update) * kept_mask[:, None]).astype(
        jnp.bfloat16
    )
    out_scale = float(full_width) ** (-0.5)
    partial_value = lax.dot_general(
        lax.all_gather(calib, "rows", axis=0, tiled=True),
        pruned_weight,
        (((1,), (1,)), ((), ())),
        preferred_element_type=jnp.float32,
    )
    token_count = partial_value.shape[0]
    own_rows = (
        lax.psum_scatter(partial_value, "mp", scatter_dimension=0, tiled=True) * out_scale
    ).astype(jnp.bfloat16)
    gram_term = lax.dot_general(
        own_rows,
        lax.all_gather(own_rows, "rows", axis=1, tiled=True),
        (((0,), (0,)), ((), ())),
        preferred_element_type=jnp.float32,
    )
    gram_block = (
        lax.psum_scatter(
            gram_term.astype(jnp.bfloat16), "mp", scatter_dimension=1, tiled=True
        ).astype(jnp.float32)
        / token_count
    )
    return (pruned_weight, gram_block)


def solution(mesh):
    return jax.shard_map(
        shards,
        mesh=mesh,
        in_specs=(P("rows", "mp"), P("rows", "mp"), P("rows", "mp"), P()),
        out_specs=(P("rows", "mp"), P("rows", "mp")),
        check_vma=False,
    )
```

profile of v0, /device:TPU:0, one launch (start us, length us, event | category | flops | bytes accessed | tf_op | source)
XLA Modules:
  0.0 823.5 jit_solution(16125952968231039749)
XLA Ops:
  13.0 4.4 constant_dynamic-slice_fusion.1
  35.9 75.9 %all-reduce.5.cloned.1.call-done = f32[1024,896]{0,1:T(8,128)} async-done(((f32[1024,896]{0,1:T(8,128)}), f32[1024,896]{0,1:T(8,128)}) %all-reduce.5.cloned.1.call-update) | async-done | bytes 3670032 | tf_op jit(solution)/shard_map/psum | solution.py:30
  137.3 116.8 %all-reduce.7.cloned.1.call-done = f32[896,896]{0,1:T(8,128)} async-done(((f32[896,896]{0,1:T(8,128)}), f32[896,896]{0,1:T(8,128)}) %all-reduce.7.cloned.1.call-update) | async-done | bytes 3211280 | tf_op jit(solution)/shard_map/psum | solution.py:44
  254.1 4.7 copy.21
  262.7 11.7 %cholesky.195 = f32[128,128]{1,0:T(8,128)S(1)} custom-call(f32[128,128]{1,0:T(8,128)S(1)} %cholesky.502), custom_call_target="Cholesky" | custom-call | tf_op jit(solution)/shard_map/jit(cholesky)/cholesky | solution.py:45
  274.7 9.8 %custom-call.56 = f32[1,128,128]{1,2,0:T(8,128)S(1)} custom-call(f32[1,128,128]{2,1,0:T(8,128)S(1)} %get-tuple-element.55), custom_call_target="InvertDiagBlocksLowerTriangular" | custom-call | tf_op jit(solution)/shard_map/jit(cholesky)/cholesky | solution.py:45
  288.2 11.7 %cholesky.216 = f32[128,128]{1,0:T(8,128)S(1)} custom-call(f32[128,128]{1,0:T(8,128)S(1)} %cholesky.506), custom_call_target="Cholesky" | custom-call | tf_op jit(solution)/shard_map/jit(cholesky)/cholesky | solution.py:45
  301.3 10.2 %custom-call.57 = f32[1,128,128]{1,2,0:T(8,128)S(1)} custom-call(f32[1,128,128]{2,1,0:T(8,128)S(1)} %get-tuple-element.52), custom_call_target="InvertDiagBlocksLowerTriangular" | custom-call | tf_op jit(solution)/shard_map/jit(cholesky)/cholesky | solution.py:45
  315.2 13.2 %cholesky.411 = f32[128,128]{1,0:T(8,128)} custom-call(f32[128,128]{1,0:T(8,128)} %cholesky.511), custom_call_target="Cholesky" | custom-call | tf_op jit(solution)/shard_map/jit(cholesky)/cholesky | solution.py:45
  330.5 11.3 %custom-call.58 = f32[1,128,128]{1,2,0:T(8,128)} custom-call(f32[1,128,128]{2,1,0:T(8,128)} %get-tuple-element.49), custom_call_target="InvertDiagBlocksLowerTriangular" | custom-call | tf_op jit(solution)/shard_map/jit(cholesky)/cholesky | solution.py:45
  344.8 12.5 %cholesky.430 = f32[128,128]{1,0:T(8,128)} custom-call(f32[128,128]{1,0:T(8,128)S(1)} %cholesky.516), custom_call_target="Cholesky" | custom-call | tf_op jit(solution)/shard_map/jit(cholesky)/cholesky | solution.py:45
  358.9 10.4 %custom-call.59 = f32[1,128,128]{1,2,0:T(8,128)} custom-call(f32[1,128,128]{2,1,0:T(8,128)S(1)} %get-tuple-element.46), custom_call_target="InvertDiagBlocksLowerTriangular" | custom-call | tf_op jit(solution)/shard_map/jit(cholesky)/cholesky | solution.py:45
  372.2 11.7 %cholesky.449 = f32[128,128]{1,0:T(8,128)S(1)} custom-call(f32[128,128]{1,0:T(8,128)S(1)} %cholesky.521), custom_call_target="Cholesky" | custom-call | tf_op jit(solution)/shard_map/jit(cholesky)/cholesky | solution.py:45
  384.6 9.8 %custom-call.60 = f32[1,128,128]{1,2,0:T(8,128)S(1)} custom-call(f32[1,128,128]{2,1,0:T(8,128)S(1)} %get-tuple-element.43), custom_call_target="InvertDiagBlocksLowerTriangular" | custom-call | tf_op jit(solution)/shard_map/jit(cholesky)/cholesky | solution.py:45
  396.3 12.1 %cholesky.469 = f32[128,128]{1,0:T(8,128)S(1)} custom-call(f32[128,128]{1,0:T(8,128)S(1)} %cholesky.526), custom_call_target="Cholesky" | custom-call | tf_op jit(solution)/shard_map/jit(cholesky)/cholesky | solution.py:45
  409.1 9.8 %custom-call.61 = f32[1,128,128]{1,2,0:T(8,128)S(1)} custom-call(f32[1,128,128]{2,1,0:T(8,128)S(1)} %get-tuple-element.40), custom_call_target="InvertDiagBlocksLowerTriangular" | custom-call | tf_op jit(solution)/shard_map/jit(cholesky)/cholesky | solution.py:45
  420.4 11.7 %cholesky.487 = f32[128,128]{1,0:T(8,128)S(1)} custom-call(f32[128,128]{1,0:T(8,128)S(1)} %convolution_subtract_fusion.13), custom_call_target="Cholesky" | custom-call | tf_op jit(solution)/shard_map/jit(cholesky)/cholesky | solution.py:45
  439.3 24.8 %while.1 = (s32[]{:T(128)}, f32[896,896]{1,0:T(8,128)}, s32[7,2]{0,1:T(2,128)S(1)}, f32[7,128,128]{2,1,0:T(8,128)}, s32[]{:T(128)}) while((s32[]{:T(128)}, f32[896,896]{1,0:T(8,128)}, s32[7,2]{0,1:T(2,128)S(1)}, f32[7,128,128]{2,1,0:T(8,128)}, s32[]{:T(128)}) %tuple.62), condition=%wide.while_cond, body=%wide.while_body.sunk | while | flops 2 | bytes 132705 | solution.py:11
  439.9 2.9 bitcast_dynamic-update-slice_fusion.2
  443.5 2.9 bitcast_dynamic-update-slice_fusion.2
  447.0 2.9 bitcast_dynamic-update-slice_fusion.2
  450.6 2.9 bitcast_dynamic-update-slice_fusion.2
  454.2 2.9 bitcast_dynamic-update-slice_fusion.2
  457.7 2.9 bitcast_dynamic-update-slice_fusion.2
  464.1 69.7 %custom-call.62 = f32[7,128,128]{1,2,0:T(8,128)S(1)} custom-call(f32[7,128,128]{2,1,0:T(8,128)} %get-tuple-element.9), custom_call_target="InvertDiagBlocksLowerTriangular" | custom-call | tf_op jit(solution)/shard_map/triangular_solve | solution.py:11
  567.2 18.1 %multiply_convert_fusion = bf16[1024,2048]{1,0:T(8,128)(2,1)} fusion(bf16[1024,2048]{1,0:T(8,128)(2,1)} %param.5, f32[1024]{0:T(1024)S(1)} %convert_subtract_fusion, f32[896,1024]{1,0:T(8,128)} %constant_dynamic-update-slice_fusion.22, bf16[896,2048]{1,0:T(8,128)(2,1)} %all-reduce.9.cloned.1.call-done), kind=kOutput, calls=%fused_computation.4 | convolution fusion | flops 22556966912 | bytes 15732736 | tf_op jit(solution)/shard_map/dot_general | solution.py:47
  585.3 6.5 convolution_bitcast_fusion
  591.9 30.3 %reduce-scatter.3.cloned.1.call-done = f32[128,1024]{0,1:T(8,128)} async-done(((f32[512,1024]{0,1:T(8,128)}), f32[128,1024]{0,1:T(8,128)}) %reduce-scatter.3.cloned.1.call-update) | async-done | bytes 524304 | tf_op jit(solution)/shard_map/reduce_scatter | solution.py:66
  624.1 49.8 %all-gather.5.cloned.1.call-done = bf16[128,8192]{0,1:T(8,128)(2,1)} async-done(((bf16[128,1024]{0,1:T(8,128)(2,1)}), bf16[128,8192]{0,1:T(8,128)(2,1)}) %all-gather.5.cloned.1.call-update) | async-done | bytes 2097168 | tf_op jit(solution)/shard_map/all_gather | solution.py:70
  673.9 11.9 %convolution_convert_fusion = bf16[1024,8192]{1,0:T(8,128)(2,1)} fusion(bf16[128,1024]{0,1:T(8,128)(2,1)} %multiply_convert_fusion.8, bf16[128,8192]{0,1:T(8,128)(2,1)} %all-gather.5.cloned.1.call-done), kind=kOutput, calls=%fused_computation.2 | convolution fusion | flops 2155872256 | bytes 19136512 | tf_op jit(solution)/shard_map/dot_general | solution.py:68
  685.8 123.6 %reduce-scatter.5.cloned.1.call-done = bf16[1024,2048]{1,0:T(8,128)(2,1)} async-done(((bf16[1024,8192]{1,0:T(8,128)(2,1)}), bf16[1024,2048]{1,0:T(8,128)(2,1)}) %reduce-scatter.5.cloned.1.call-update) | async-done | bytes 4194320 | tf_op jit(solution)/shard_map/reduce_scatter | solution.py:75
  809.4 6.8 convert_multiply_fusion
  (171 shorter events, 113.2 us)
Async XLA Ops:
  7.2 104.6 %all-reduce.5.cloned.1.call-start = ((), (), s32[]{:S(2)}) async-start(), calls=%async_computation.2 | async-start | bytes 7340032 | tf_op jit(solution)/shard_map/psum | solution.py:30
  20.4 5.1 copy-start.5
  21.4 4.9 copy-start.6
  22.5 4.7 copy-start.7
  23.5 4.5 copy-start.8
  24.5 4.4 copy-start.9
  25.5 4.2 copy-start.10
  25.5 5.0 copy-start.11
  31.4 222.7 %all-reduce.7.cloned.1.call-start = ((), (), s32[]{:S(2)}) async-start(), calls=%async_computation.3 | async-start | bytes 6422528 | tf_op jit(solution)/shard_map/psum | solution.py:44
  120.6 1.7 copy-start.4
  122.3 444.9 %all-reduce.9.cloned.1.call-start = ((), (), s32[]{:S(2)}) async-start(), calls=%async_computation.4 | async-start | bytes 7340032 | tf_op jit(solution)/shard_map/psum | solution.py:41
  132.5 4.7 copy-start.13
  136.6 448.7 %all-gather.3.cloned.1.call-start = ((), (), s32[]{:S(2)}) async-start(), calls=%async_computation.5 | async-start | bytes 2359296 | tf_op jit(solution)/shard_map/all_gather | solution.py:59
  137.1 485.1 %reduce-scatter.3.cloned.1.call-start = ((), (), s32[]{:S(2)}) async-start(), calls=%async_computation.6 | async-start | bytes 2621440 | tf_op jit(solution)/shard_map/reduce_scatter | solution.py:66
  254.1 4.7 copy-start
  261.0 1.7 copy-start.3
  287.4 0.7 copy-start.12
  533.9 4.2 copy-start.1
  537.4 3.3 copy-start.2
  591.8 82.0 %all-gather.5.cloned.1.call-start = ((), (), s32[]{:S(2)}) async-start(), calls=%async_computation.7 | async-start | bytes 2359296 | tf_op jit(solution)/shard_map/all_gather | solution.py:70
  624.0 185.4 %reduce-scatter.5.cloned.1.call-start = ((), (), s32[]{:S(2)}) async-start(), calls=%async_computation.8 | async-start | bytes 20971520 | tf_op jit(solution)/shard_map/reduce_scatter | solution.py:75
Sparse Core Ops, SparseCore 0:
  31.5 80.1 all-reduce.4
  122.4 131.6 all-reduce.6
  258.3 141.9 all-reduce.8
  402.3 48.7 all-gather.2
  592.0 30.2 reduce-scatter.2
  624.8 49.0 all-gather.4
  686.0 123.4 reduce-scatter.4
where the time goes:
time: 830 us; the launch traced here: 824 us
  waiting for transfers between devices  397 us (48%)
  other arithmetic  265 us (32%)
  matrix products  79.4 us (10%)
  local copies, waits for them, and re-layouts  53 us (6%)
  between operations  28.5 us (3%)
    another operation x27, other arithmetic, shards(): chol_lower = jnp.linalg.cholesky(inverse_square)  153 us
    reduce_scatter x1, waiting for transfers between devices, shards(): lax.psum_scatter(gram_term.astype(jnp.bfloat16), 'mp', scatter_dimension=...  124 us
    psum x1, waiting for transfers between devices, shards(): inverse_square = lax.psum(jnp.concatenate(inverse_parts, axis=0), 'rows')  117 us
    psum x1, waiting for transfers between devices, shards(): columns = lax.psum(jnp.concatenate(col_pieces, axis=1), 'mp')  75.9 us
    another operation x3, other arithmetic, spd_solve(): lax.linalg.triangular_solve(chol_lower, forward, left_side=True, lower=Tr...  72.3 us
    all_gather x1, waiting for transfers between devices, shards(): lax.all_gather(own_rows, 'rows', axis=1, tiled=True)  49.8 us
    reduce_scatter x1, waiting for transfers between devices, shards(): lax.psum_scatter(partial_value, 'mp', scatter_dimension=0, tiled=True)  30.3 us
    another operation x21, local copies, waits for them, and re-layouts  24.8 us
  transfers between devices with their start and end apart: 7, of which 5 were waited for; matrix products, arithmetic and copies ran while one was open for 41% of the time, Pallas kernels for 0%

commit v1 on v0

--- a/solution.py
+++ b/solution.py
@@ -4,6 +4,12 @@
 from jax.sharding import PartitionSpec as P
 
 BLOCK = 128
+
+
+def add_all(x, mesh_axis):
+    parts = lax.all_gather(x, mesh_axis, axis=0, tiled=False)
+    acc = parts.sum(axis=0)
+    return acc
 
 
 def spd_solve(chol_lower, right_side):
@@ -41,7 +47,7 @@
     kept_rows = lax.psum(jnp.concatenate(weight_parts, axis=0).astype(jnp.bfloat16), "rows").astype(
         jnp.float32
     )
-    inverse_square = lax.psum(jnp.concatenate(inverse_parts, axis=0), "rows")
+    inverse_square = add_all(jnp.concatenate(inverse_parts, axis=0), "rows")
     chol_lower = jnp.linalg.cholesky(inverse_square)
     factors = spd_solve(chol_lower, columns.T)
     update = lax.dot_general(

time: 830 us -> 1230 us (1.48)
  waiting for transfers between devices: 397 us -> 758 us
  local copies, waits for them, and re-layouts: 53 us -> 78.5 us
    all_gather x0 -> x1, waiting for transfers between devices: none -> 476 us  [add_all(): parts = lax.all_gather(x, mesh_axis, axis=0, tiled=False)]
    psum x1 -> x0, waiting for transfers between devices: 117 us -> none  [shards(): inverse_square = lax.psum(jnp.concatenate(inverse_parts, axis=0), 'rows')]
    all_gather x0 -> x1, local copies, waits for them, and re-layouts: none -> 27.1 us  [add_all(): parts = lax.all_gather(x, mesh_axis, axis=0, tiled=False)]
  transfers between devices with their start and end apart: 7 -> 7, of which waited for: 5 -> 5; matrix products, arithmetic and copies ran while one was open for 41% -> 31% of each run, Pallas kernels for 0% -> 0%
where the time goes in v1:
time: 1230 us; the launch traced here: 1220 us
  waiting for transfers between devices  758 us (62%)
  other arithmetic  277 us (23%)
  matrix products  79.4 us (6%)
  local copies, waits for them, and re-layouts  78.5 us (6%)
  between operations  28 us (2%)
    all_gather x1, waiting for transfers between devices, add_all(): parts = lax.all_gather(x, mesh_axis, axis=0, tiled=False)  476 us
    another operation x27, other arithmetic, shards(): chol_lower = jnp.linalg.cholesky(inverse_square)  153 us
    reduce_scatter x1, waiting for transfers between devices, shards(): lax.psum_scatter(gram_term.astype(jnp.bfloat16), 'mp', scatter_dimension=...  124 us
    psum x1, waiting for transfers between devices, shards(): columns = lax.psum(jnp.concatenate(col_pieces, axis=1), 'mp')  75.9 us
    another operation x3, other arithmetic, spd_solve(): lax.linalg.triangular_solve(chol_lower, forward, left_side=True, lower=Tr...  72.3 us
    all_gather x1, waiting for transfers between devices, shards(): lax.all_gather(own_rows, 'rows', axis=1, tiled=True)  49.8 us
    reduce_scatter x1, waiting for transfers between devices, shards(): lax.psum_scatter(partial_value, 'mp', scatter_dimension=0, tiled=True)  31.6 us
    all_gather x1, local copies, waits for them, and re-layouts, add_all(): parts = lax.all_gather(x, mesh_axis, axis=0, tiled=False)  27.1 us
  transfers between devices with their start and end apart: 7, of which 5 were waited for; matrix products, arithmetic and copies ran while one was open for 31% of the time, Pallas kernels for 0%

profile of v1, /device:TPU:0, one launch (start us, length us, event | category | flops | bytes accessed | tf_op | source)
XLA Modules:
  0.0 1220.5 jit_solution(3139701847563368533)
XLA Ops:
  12.8 4.4 constant_dynamic-slice_fusion.1
  35.5 75.9 %all-reduce.4.cloned.1.call-done = f32[1024,896]{0,1:T(8,128)} async-done(((f32[1024,896]{0,1:T(8,128)}), f32[1024,896]{0,1:T(8,128)}) %all-reduce.4.cloned.1.call-update) | async-done | bytes 3670032 | tf_op jit(solution)/shard_map/psum | solution.py:36
  137.0 476.1 %all-gather.9.cloned.1.call-done = f32[7168,896]{0,1:T(8,128)} async-done(((f32[896,896]{0,1:T(8,128)}), f32[7168,896]{0,1:T(8,128)}) %all-gather.9.cloned.1.call-update) | async-done | bytes 25690128 | tf_op jit(solution)/shard_map/all_gather | solution.py:10
  613.1 27.1 %copy.17 = f32[7168,896]{1,0:T(8,128)} copy(f32[7168,896]{0,1:T(8,128)} %all-gather.9.cloned.1.call-done) | data formatting | bytes 51380224 | tf_op jit(solution)/shard_map/all_gather | solution.py:10
  640.2 11.6 reduce_sum.9
  651.9 3.2 copy.16
  659.0 11.7 cholesky.195
  670.9 9.8 custom-call.56
  684.4 11.7 cholesky.216
  697.5 10.2 custom-call.57
  711.4 13.2 %cholesky.411 = f32[128,128]{1,0:T(8,128)} custom-call(f32[128,128]{1,0:T(8,128)} %cholesky.511), custom_call_target="Cholesky" | custom-call | tf_op jit(solution)/shard_map/jit(cholesky)/cholesky | solution.py:51
  726.7 11.3 custom-call.58
  740.9 12.5 %cholesky.430 = f32[128,128]{1,0:T(8,128)} custom-call(f32[128,128]{1,0:T(8,128)S(1)} %cholesky.516), custom_call_target="Cholesky" | custom-call | tf_op jit(solution)/shard_map/jit(cholesky)/cholesky | solution.py:51
  755.0 10.4 custom-call.59
  768.3 11.7 cholesky.449
  780.7 9.8 custom-call.60
  792.4 12.1 cholesky.469
  805.1 9.8 custom-call.61
  816.5 11.7 cholesky.487
  835.0 24.7 %while.1 = (s32[]{:T(128)}, f32[896,896]{1,0:T(8,128)}, s32[7,2]{0,1:T(2,128)S(1)}, f32[7,128,128]{2,1,0:T(8,128)}, s32[]{:T(128)}) while((s32[]{:T(128)}, f32[896,896]{1,0:T(8,128)}, s32[7,2]{0,1:T(2,128)S(1)}, f32[7,128,128]{2,1,0:T(8,128)}, s32[]{:T(128)}) %tuple.62), condition=%wide.while_cond, body=%wide.while_body.sunk | while | flops 2 | bytes 132705 | solution.py:17
  835.7 2.9 bitcast_dynamic-update-slice_fusion.2
  839.3 2.9 bitcast_dynamic-update-slice_fusion.2
  842.8 2.9 bitcast_dynamic-update-slice_fusion.2
  853.4 2.9 bitcast_dynamic-update-slice_fusion.2
  859.8 69.7 %custom-call.62 = f32[7,128,128]{1,2,0:T(8,128)S(1)} custom-call(f32[7,128,128]{2,1,0:T(8,128)} %get-tuple-element.9), custom_call_target="InvertDiagBlocksLowerTriangular" | custom-call | tf_op jit(solution)/shard_map/triangular_solve | solution.py:17
  962.9 18.1 %multiply_convert_fusion = bf16[1024,2048]{1,0:T(8,128)(2,1)} fusion(bf16[1024,2048]{1,0:T(8,128)(2,1)} %param.5, f32[1024]{0:T(1024)S(1)} %convert_subtract_fusion, f32[896,1024]{1,0:T(8,128)} %constant_dynamic-update-slice_fusion.22, bf16[896,2048]{1,0:T(8,128)(2,1)} %all-reduce.6.cloned.1.call-done), kind=kOutput, calls=%fused_computation.4 | convolution fusion | flops 22556966912 | bytes 15732736 | tf_op jit(solution)/shard_map/dot_general | solution.py:53
  981.0 6.5 convolution_bitcast_fusion
  987.6 31.6 %reduce-scatter.3.cloned.1.call-done = f32[128,1024]{0,1:T(8,128)} async-done(((f32[512,1024]{0,1:T(8,128)}), f32[128,1024]{0,1:T(8,128)}) %reduce-scatter.3.cloned.1.call-update) | async-done | bytes 524304 | tf_op jit(solution)/shard_map/reduce_scatter | solution.py:72
  1021.0 49.8 %all-gather.7.cloned.1.call-done = bf16[128,8192]{0,1:T(8,128)(2,1)} async-done(((bf16[128,1024]{0,1:T(8,128)(2,1)}), bf16[128,8192]{0,1:T(8,128)(2,1)}) %all-gather.7.cloned.1.call-update) | async-done | bytes 2097168 | tf_op jit(solution)/shard_map/all_gather | solution.py:76
  1070.9 11.9 convolution_convert_fusion
  1082.8 123.6 %reduce-scatter.5.cloned.1.call-done = bf16[1024,2048]{1,0:T(8,128)(2,1)} async-done(((bf16[1024,8192]{1,0:T(8,128)(2,1)}), bf16[1024,2048]{1,0:T(8,128)(2,1)}) %reduce-scatter.5.cloned.1.call-update) | async-done | bytes 4194320 | tf_op jit(solution)/shard_map/reduce_scatter | solution.py:81
  1206.4 6.8 convert_multiply_fusion
  (171 shorter events, 118.7 us)
Async XLA Ops:
  7.2 104.3 %all-reduce.4.cloned.1.call-start = ((), (), s32[]{:S(2)}) async-start(), calls=%async_computation.2 | async-start | bytes 7340032 | tf_op jit(solution)/shard_map/psum | solution.py:36
  20.2 5.1 copy-start.4
  21.2 4.9 copy-start.5
  22.3 4.7 copy-start.6
  23.3 4.5 copy-start.7
  24.3 4.4 copy-start.8
  25.3 4.2 copy-start.9
  25.3 5.0 copy-start.10
  31.2 581.9 %all-gather.9.cloned.1.call-start = ((), (), s32[]{:S(2)}) async-start(), calls=%async_computation.8 | async-start | bytes 28901376 | tf_op jit(solution)/shard_map/all_gather | solution.py:10
  120.3 1.7 copy-start.3
  122.0 840.9 %all-reduce.6.cloned.1.call-start = ((), (), s32[]{:S(2)}) async-start(), calls=%async_computation.3 | async-start | bytes 7340032 | tf_op jit(solution)/shard_map/psum | solution.py:47
  132.2 4.7 copy-start.12
  136.2 844.7 %all-gather.5.cloned.1.call-start = ((), (), s32[]{:S(2)}) async-start(), calls=%async_computation.4 | async-start | bytes 2359296 | tf_op jit(solution)/shard_map/all_gather | solution.py:65
  136.8 882.4 %reduce-scatter.3.cloned.1.call-start = ((), (), s32[]{:S(2)}) async-start(), calls=%async_computation.5 | async-start | bytes 2621440 | tf_op jit(solution)/shard_map/reduce_scatter | solution.py:72
  657.3 1.7 copy-start.2
  683.7 0.7 copy-start.11
  929.5 4.2 copy-start
  933.1 3.3 copy-start.1
  987.5 83.3 %all-gather.7.cloned.1.call-start = ((), (), s32[]{:S(2)}) async-start(), calls=%async_computation.6 | async-start | bytes 2359296 | tf_op jit(solution)/shard_map/all_gather | solution.py:76
  1021.0 185.4 %reduce-scatter.5.cloned.1.call-start = ((), (), s32[]{:S(2)}) async-start(), calls=%async_computation.7 | async-start | bytes 20971520 | tf_op jit(solution)/shard_map/reduce_scatter | solution.py:81
Sparse Core Ops, SparseCore 0:
  31.3 80.0 all-reduce.3
  122.1 490.9 all-gather.8
  617.4 142.9 all-reduce.5
  762.3 48.9 all-gather.4
  987.6 31.4 reduce-scatter.2
  1021.7 49.0 all-gather.6
  1082.9 123.4 reduce-scatter.4
